TPU v7x, 32 devices: a whole 2x2x4 slice. The times are simulated.
32 devices in a mesh: az: 16 (over z, x, core), el: 2 (over y).
Axes of the slice: x: 2, y: 2, z: 4, core: 2. Of those that a mesh axis runs over, the one named last changes fastest.
Arguments:
- raw_sweeps: bfloat16 [4, 1, 24, 96, 256], P('el', None, None, 'az'), may hold values from -6 to 6
- sweep_ids: int32 [4], P('el'), may hold values from 0 to 3, each once
- elevation_embed: float32 [4, 128], replicated, may hold values from -3 to 3
- input_proj: bfloat16 [24, 128], replicated, may hold values from -0.875 to 0.875
- first_kernel: bfloat16 [3, 3, 128, 128], replicated, may hold values from -0.1875 to 0.1875
- second_kernel: bfloat16 [3, 3, 128, 128], replicated, may hold values from -0.1875 to 0.1875
- join_weight: bfloat16 [2, 128, 128], P('el'), may hold values from -0.375 to 0.375
- head_weight: bfloat16 [12, 128], replicated, may hold values from -0.5 to 0.5
- cotangent: bfloat16 [1, 12, 96, 256], P(None, None, 'az'), may hold values from -6 to 6
Outputs:
- prediction: float32 [1, 12, 96, 256], P(None, None, 'az')
- join_grad: float32 [2, 128, 128], P('el')
- first_kernel_gradient: float32 [3, 3, 128, 128], replicated
- second_kernel_gradient: float32 [3, 3, 128, 128], replicated
- input_grad: float32 [24, 128], replicated
- embed_grad: float32 [4, 128], replicated
Inputs may be any that keep to these rules, and one draw needn't show every extreme that they name: `sweep_ids`: each sweep fills exactly one slot.
All inputs are finite; a program needn't handle non-finite values.
Results may differ from a plain program's by a relative error of at most 0.023.
Values may be sent and summed in bfloat16 or wider, within the bound.
A program may use at most 64 MiB of HBM per device.

v0:
```python
import math
import jax
import jax.numpy as jnp
from jax import lax
from jax.sharding import PartitionSpec as P

CHANNELS = 128
FIRST_DILATION = 1
SECOND_DILATION = 2
precise = lax.Precision.HIGHEST


def padded_2(block, sides, width):
    for axis, dim in sides:
        count = lax.axis_size(axis)
        forward = [(i, i + 1) for i in range(count - 1)]
        forward.append((count - 1, 0))
        backward = [(target, source) for source, target in forward]
        low = lax.ppermute(
            lax.slice_in_dim(block, block.shape[dim] - width, None, axis=dim), axis, forward
        )
        high = lax.ppermute(lax.slice_in_dim(block, 0, width, axis=dim), axis, backward)
        block = jnp.concatenate([low, block, high], axis=dim)
    return block


def silu_slope(values):
    logistic = jax.nn.sigmoid(values)
    return logistic * (1.0 + values * (1.0 - logistic))


def range_padding(source, dilate):
    return jnp.pad(source, ((0, 0), (0, 0), (0, 0), (dilate, dilate)))


def convolve_partial(padded, kernel, dilate):
    return lax.conv_general_dilated(
        padded,
        kernel,
        (1, 1),
        "VALID",
        rhs_dilation=(dilate, dilate),
        dimension_numbers=("NCHW", "HWIO", "NCHW"),
        preferred_element_type=jnp.float32,
    )


def reversed_kernel(kernel):
    return jnp.flip(kernel, (0, 1)).transpose(0, 1, 3, 2)


def kernel_gradient_of(padded, upstream, dilate):
    ray_count = upstream.shape[2]
    gate_count = upstream.shape[3]
    tap_rows = []
    for tap_row in range(3):
        tap_line = []
        for tap_column in range(3):
            window = padded[
                :,
                :,
                tap_row * dilate : tap_row * dilate + ray_count,
                tap_column * dilate : tap_column * dilate + gate_count,
            ]
            tap_line.append(
                jnp.einsum("niar,noar->io", window, upstream, preferred_element_type=jnp.float32)
            )
        tap_rows.append(jnp.stack(tap_line))
    return jnp.stack(tap_rows)


def activate(source):
    return jax.nn.silu(source.astype(jnp.float32)).astype(jnp.bfloat16)


def shards(
    raw_sweeps,
    sweep_ids,
    elevation_embed,
    input_proj,
    first_kernel,
    second_kernel,
    join_weight,
    head_weight,
    cotangent,
):
    brain_float_half = jnp.bfloat16
    sweep_total = elevation_embed.shape[0]
    onehot = (sweep_ids[:, None] == jnp.arange(sweep_total, dtype=jnp.int32)[None, :]).astype(
        jnp.float32
    )
    bias_rows = jnp.dot(onehot, elevation_embed, precision=precise)
    group_bias = jnp.sum(bias_rows, axis=0)
    input_state = jnp.einsum(
        "jbiar,ic->bcar", raw_sweeps, input_proj, preferred_element_type=jnp.float32
    )
    input_state = (input_state + group_bias[None, :, None, None]).astype(brain_float_half)
    input_activation = activate(input_state)
    padded_input = range_padding(
        padded_2(input_activation, (("az", 2),), FIRST_DILATION), FIRST_DILATION
    )
    hidden_state = (
        input_state.astype(jnp.float32)
        + convolve_partial(padded_input, first_kernel, FIRST_DILATION)
    ).astype(brain_float_half)
    hidden_activation = activate(hidden_state)
    padded_hidden = range_padding(
        padded_2(hidden_activation, (("az", 2),), SECOND_DILATION), SECOND_DILATION
    )
    final_state = (
        hidden_state.astype(jnp.float32)
        + convolve_partial(padded_hidden, second_kernel, SECOND_DILATION)
    ).astype(brain_float_half)
    group_weight = join_weight[0]
    empty_sum = jnp.zeros((CHANNELS,) + final_state.shape[:1] + final_state.shape[2:], jnp.float32)
    joined_all = (
        empty_sum
        + jnp.einsum(
            "gbiar,gio->obar",
            lax.all_gather(final_state[None], "el", axis=0, tiled=True),
            lax.all_gather(join_weight, "el", axis=0, tiled=True),
            preferred_element_type=jnp.float32,
        )
    ).astype(brain_float_half)
    prediction = jnp.einsum(
        "lc,cbar->blar", head_weight, joined_all, preferred_element_type=jnp.float32
    )
    ray_total = final_state.shape[2] * lax.axis_size("az")
    grad_scale = 1.0 / math.sqrt(
        lax.axis_size("el") * final_state.shape[0] * ray_total * final_state.shape[3]
    )
    joined_back = jnp.einsum(
        "lc,blar->bcar", head_weight, cotangent, preferred_element_type=jnp.float32
    ).astype(brain_float_half)
    join_local = jnp.einsum(
        "biar,boar->io", final_state, joined_back, preferred_element_type=jnp.float32
    )
    join_total = lax.psum(join_local, "az")
    grad_two = jnp.einsum(
        "io,boar->biar", group_weight, joined_back, preferred_element_type=jnp.float32
    )
    final_upstream_gradient = grad_two.astype(brain_float_half)
    second_kernel_partial = kernel_gradient_of(
        padded_hidden, final_upstream_gradient, SECOND_DILATION
    )
    second_border_rays = range_padding(
        padded_2(final_upstream_gradient, (("az", 2),), SECOND_DILATION), SECOND_DILATION
    )
    second_backward_pass = convolve_partial(
        second_border_rays, reversed_kernel(second_kernel), SECOND_DILATION
    )
    grad_one = grad_two + second_backward_pass * silu_slope(hidden_state.astype(jnp.float32))
    hidden_upstream_gradient = grad_one.astype(brain_float_half)
    first_kernel_partial = kernel_gradient_of(
        padded_input, hidden_upstream_gradient, FIRST_DILATION
    )
    first_border_rays = range_padding(
        padded_2(hidden_upstream_gradient, (("az", 2),), FIRST_DILATION), FIRST_DILATION
    )
    first_backward_pass = convolve_partial(
        first_border_rays, reversed_kernel(first_kernel), FIRST_DILATION
    )
    grad_zero = (
        grad_one + first_backward_pass * silu_slope(input_state.astype(jnp.float32))
    ).astype(brain_float_half)
    input_local = jnp.einsum(
        "jbiar,bcar->ic", raw_sweeps, grad_zero, preferred_element_type=jnp.float32
    )
    column_sum = jnp.sum(grad_zero.astype(jnp.float32), axis=(0, 2, 3))
    slot_terms = jnp.broadcast_to(column_sum[None, :], (raw_sweeps.shape[0], column_sum.shape[0]))
    embed_local = jnp.dot(onehot.T, slot_terms, precision=precise)
    second_total, first_total, input_total, embed_total = lax.psum(
        (second_kernel_partial, first_kernel_partial, input_local, embed_local), ("az", "el")
    )
    return (
        prediction,
        join_total[None] * grad_scale,
        first_total * grad_scale,
        second_total * grad_scale,
        input_total * grad_scale,
        embed_total * grad_scale,
    )


def solution(mesh):
    in_specs = (
        P("el", None, None, "az", None),
        P("el"),
        P(),
        P(),
        P(),
        P(),
        P("el", None, None),
        P(),
        P(None, None, "az", None),
    )
    out_specs = (P(None, None, "az", None), P("el", None, None), P(), P(), P(), P())
    return jax.shard_map(shards, mesh=mesh, in_specs=in_specs, out_specs=out_specs, check_vma=False)
```

profile of v0, /device:TPU:0, one launch (start us, length us, event | category | flops | bytes accessed | tf_op | source)
XLA Modules:
  0.0 342.1 jit_solution(14312674388534561637)
XLA Ops:
  7.2 1.0 convert_reduce_fusion.1
  8.2 0.9 convolution_reduce_fusion
  9.1 1.9 fusion.30
  11.6 5.0 %collective-permute-start.1 = (bf16[1,128,1,256]{1,3,2,0:T(8,128)(2,1)S(1)}, bf16[1,128,1,256]{1,3,2,0:T(8,128)(2,1)S(1)}, u32[]{:S(2)}, u32[]{:S(2)}) collective-permute-start(bf16[1,128,1,256]{1,3,2,0:T(8,128)(2,1)S(1)} %get-tuple-element.42), channel_id=1, source_target_pairs={{2,0},{4,2},{6,4},{8,6},{10,8},{12,10},{14,12},{16,14},{18,16},{20... | collective-permute-start | bytes 196616 | tf_op jit(solution)/shard_map/ppermute | solution.py:22
  16.9 1.2 fusion.177
  18.2 4.4 %collective-permute-start.5 = (bf16[1,128,2,256]{1,3,2,0:T(8,128)(2,1)S(1)}, bf16[1,128,2,256]{1,3,2,0:T(8,128)(2,1)S(1)}, u32[]{:S(2)}, u32[]{:S(2)}) collective-permute-start(bf16[1,128,2,256]{1,3,2,0:T(8,128)(2,1)S(1)} %get-tuple-element.44), channel_id=1, source_target_pairs={{2,0},{4,2},{6,4},{8,6},{10,8},{12,10},{14,12},{16,14},{18,16},{20... | collective-permute-start | bytes 393224 | tf_op jit(solution)/shard_map/ppermute | solution.py:22
  22.6 4.7 %all_gather.7 = bf16[2,128,128]{2,1,0:T(8,128)(2,1)} all-gather(bf16[1,128,128]{2,1,0:T(8,128)(2,1)S(1)} %copy-done.10), channel_id=1, replica_groups=mesh['az'=16,'el'=2] {'el'}, dimensions={0}, use_global_device_ids=true | all-gather | bytes 98304 | tf_op jit(solution)/shard_map/all_gather | solution.py:121
  28.6 1.1 convolution_select_fusion.3
  29.9 1.0 reshape.182
  32.4 1.1 convolution_select_fusion.1
  33.7 1.0 reshape.186
  34.6 3.1 fusion.170
  38.0 0.9 convolution_bitcast_fusion.6
  41.6 4.4 %collective-permute-start.7 = (bf16[1,128,1,256]{1,3,2,0:T(8,128)(2,1)S(1)}, bf16[1,128,1,256]{1,3,2,0:T(8,128)(2,1)S(1)}, u32[]{:S(2)}, u32[]{:S(2)}) collective-permute-start(bf16[1,128,1,256]{1,3,2,0:T(8,128)(2,1)S(1)} %get-tuple-element.38), channel_id=1, source_target_pairs={{2,0},{4,2},{6,4},{8,6},{10,8},{12,10},{14,12},{16,14},{18,16},{20... | collective-permute-start | bytes 196616 | tf_op jit(solution)/shard_map/ppermute | solution.py:22
  46.0 4.4 %collective-permute-start.3 = (bf16[1,128,2,256]{1,3,2,0:T(8,128)(2,1)S(1)}, bf16[1,128,2,256]{1,3,2,0:T(8,128)(2,1)S(1)}, u32[]{:S(2)}, u32[]{:S(2)}) collective-permute-start(bf16[1,128,2,256]{1,3,2,0:T(8,128)(2,1)S(1)} %get-tuple-element.40), channel_id=1, source_target_pairs={{2,0},{4,2},{6,4},{8,6},{10,8},{12,10},{14,12},{16,14},{18,16},{20... | collective-permute-start | bytes 393224 | tf_op jit(solution)/shard_map/ppermute | solution.py:22
  52.6 1.1 convolution_select_fusion
  53.9 1.0 reshape.188
  54.8 2.0 convert_reduce_fusion
  57.2 37.2 %all-reduce.2 = (f32[24,128]{1,0:T(8,128)S(1)}, f32[4,128]{1,0:T(4,128)S(1)}) all-reduce(f32[24,128]{1,0:T(8,128)S(1)} %convolution_bitcast_fusion.21, f32[4,128]{1,0:T(4,128)S(1)} %fusion.135), channel_id=1, replica_groups=mesh['az'=16,'el'=2] {'az','el'}, use_global_device_ids=true, to_apply=%region_5.6 | all-reduce | flops 3584 | bytes 28672 | tf_op jit(solution)/shard_map/psum | solution.py:172
  96.4 0.9 convolution_bitcast_fusion.7
  97.3 0.9 convolution_bitcast_fusion.8
  98.3 0.9 convolution_bitcast_fusion.2
  99.2 0.9 convolution_bitcast_fusion.4
  101.5 1.1 convolution_select_fusion.2
  102.8 1.0 reshape.184
  103.8 1.2 fusion.15
  105.1 0.9 convolution_bitcast_fusion.20
  108.6 11.7 %all-gather = bf16[2,128,6,256]{3,1,2,0:T(8,128)(2,1)S(1)} all-gather(bf16[1,128,6,256]{3,1,2,0:T(8,128)(2,1)S(1)} %copy.130), channel_id=2, replica_groups=mesh['az'=16,'el'=2] {'el'}, dimensions={0}, use_global_device_ids=true | all-gather | bytes 1179648 | tf_op jit(solution)/shard_map/all_gather | solution.py:120
  121.8 70.7 %all-reduce.7.cloned.1.call-done = f32[128,128]{1,0:T(8,128)} async-done(((f32[128,128]{1,0:T(8,128)}), f32[128,128]{1,0:T(8,128)}) %all-reduce.7.cloned.1.call-update) | async-done | bytes 65552 | tf_op jit(solution)/shard_map/psum | solution.py:138
  192.5 1.5 multiply_bitcast_fusion
  193.9 138.5 %all-reduce.9.cloned.1.call-done = (f32[3,3,128,128]{3,2,1,0:T(8,128)}, f32[3,3,128,128]{3,2,1,0:T(8,128)}) async-done(((f32[3,3,128,128]{3,2,1,0:T(8,128)}, f32[3,3,128,128]{3,2,1,0:T(8,128)}), (f32[3,3,128,128]{3,2,1,0:T(8,128)}, f32[3,3,128,128]{3,2,1,0:T(8,128)})) %all-reduce.9.cloned.1.call-update) | async-done | bytes 1179664 | tf_op jit(solution)/shard_map/psum | solution.py:172
  332.4 2.0 broadcast_multiply_fusion
  (119 shorter events, 17.7 us)
Async XLA Ops:
  7.2 20.9 %copy-start = (bf16[3,3,128,128]{3,2,1,0:T(8,128)(2,1)S(1)}, bf16[3,3,128,128]{3,2,1,0:T(8,128)(2,1)}, u32[]{:S(2)}) copy-start(bf16[3,3,128,128]{3,2,1,0:T(8,128)(2,1)} %param.13) | copy-start | bytes 884740
  7.2 185.3 %all-reduce.7.cloned.1.call-start = ((), (), s32[]{:S(2)}) async-start(), calls=%async_computation | async-start | bytes 131072 | tf_op jit(solution)/shard_map/psum | solution.py:138
  9.1 7.5 %copy-start.17 = (bf16[1,12,6,256]{3,2,1,0:T(8,128)(2,1)S(1)}, bf16[1,12,6,256]{3,2,1,0:T(8,128)(2,1)}, u32[]{:S(2)}) copy-start(bf16[1,12,6,256]{3,2,1,0:T(8,128)(2,1)} %param.17) | copy-start | bytes 110596
  9.1 7.5 %copy-start.18 = (bf16[12,128]{1,0:T(8,128)(2,1)S(1)}, bf16[12,128]{1,0:T(8,128)(2,1)}, u32[]{:S(2)}) copy-start(bf16[12,128]{1,0:T(8,128)(2,1)} %param.16) | copy-start | bytes 9220
  9.1 7.8 %copy-start.10 = (bf16[1,128,128]{2,1,0:T(8,128)(2,1)S(1)}, bf16[1,128,128]{2,1,0:T(8,128)(2,1)}, u32[]{:S(2)}) copy-start(bf16[1,128,128]{2,1,0:T(8,128)(2,1)} %param.15) | copy-start | bytes 98308
  11.1 16.2 %copy-start.1 = (bf16[128,6,256]{0,2,1:T(8,128)(2,1)}, bf16[128,6,256]{0,2,1:T(8,128)(2,1)S(1)}, u32[]{:S(2)}) copy-start(bf16[128,6,256]{0,2,1:T(8,128)(2,1)S(1)} %get-tuple-element.47) | copy-start | bytes 1179652
  11.1 16.2 %collective-permute-start = (bf16[1,128,1,256]{1,3,2,0:T(8,128)(2,1)S(1)}, bf16[1,128,1,256]{1,3,2,0:T(8,128)(2,1)S(1)}, u32[]{:S(2)}, u32[]{:S(2)}) collective-permute-start(bf16[1,128,1,256]{1,3,2,0:T(8,128)(2,1)S(1)} %get-tuple-element.41), channel_id=1, source_target_pairs={{0,2},{2,4},{4,6},{6,8},{8,10},{10,12},{12,14},{14,16},{16,18},{18... | collective-permute-start | bytes 196616 | tf_op jit(solution)/shard_map/ppermute | solution.py:19
  11.6 15.7 %collective-permute-start.1 = (bf16[1,128,1,256]{1,3,2,0:T(8,128)(2,1)S(1)}, bf16[1,128,1,256]{1,3,2,0:T(8,128)(2,1)S(1)}, u32[]{:S(2)}, u32[]{:S(2)}) collective-permute-start(bf16[1,128,1,256]{1,3,2,0:T(8,128)(2,1)S(1)} %get-tuple-element.42), channel_id=1, source_target_pairs={{2,0},{4,2},{6,4},{8,6},{10,8},{12,10},{14,12},{16,14},{18,16},{20... | collective-permute-start | bytes 196616 | tf_op jit(solution)/shard_map/ppermute | solution.py:22
  18.1 12.8 %collective-permute-start.4 = (bf16[1,128,2,256]{1,3,2,0:T(8,128)(2,1)S(1)}, bf16[1,128,2,256]{1,3,2,0:T(8,128)(2,1)S(1)}, u32[]{:S(2)}, u32[]{:S(2)}) collective-permute-start(bf16[1,128,2,256]{1,3,2,0:T(8,128)(2,1)S(1)} %get-tuple-element.43), channel_id=1, source_target_pairs={{0,2},{2,4},{4,6},{6,8},{8,10},{10,12},{12,14},{14,16},{16,18},{18... | collective-permute-start | bytes 393224 | tf_op jit(solution)/shard_map/ppermute | solution.py:19
  18.2 12.7 %collective-permute-start.5 = (bf16[1,128,2,256]{1,3,2,0:T(8,128)(2,1)S(1)}, bf16[1,128,2,256]{1,3,2,0:T(8,128)(2,1)S(1)}, u32[]{:S(2)}, u32[]{:S(2)}) collective-permute-start(bf16[1,128,2,256]{1,3,2,0:T(8,128)(2,1)S(1)} %get-tuple-element.44), channel_id=1, source_target_pairs={{2,0},{4,2},{6,4},{8,6},{10,8},{12,10},{14,12},{16,14},{18,16},{20... | collective-permute-start | bytes 393224 | tf_op jit(solution)/shard_map/ppermute | solution.py:22
  27.9 0.7 copy-start.22
  31.4 1.0 copy-start.19
  39.5 1.0 copy-start.2
  40.9 9.6 %copy-start.16 = (bf16[1,128,1,256]{1,3,2,0:T(8,128)(2,1)S(1)}, bf16[1,128,1,256]{1,3,2,0:T(8,128)(2,1)}, u32[]{:S(2)}) copy-start(bf16[1,128,1,256]{1,3,2,0:T(8,128)(2,1)} %copy-done.15) | copy-start | bytes 196612
  41.5 10.5 %collective-permute-start.6 = (bf16[1,128,1,256]{1,3,2,0:T(8,128)(2,1)S(1)}, bf16[1,128,1,256]{1,3,2,0:T(8,128)(2,1)S(1)}, u32[]{:S(2)}, u32[]{:S(2)}) collective-permute-start(bf16[1,128,1,256]{1,3,2,0:T(8,128)(2,1)S(1)} %get-tuple-element.37), channel_id=1, source_target_pairs={{0,2},{2,4},{4,6},{6,8},{8,10},{10,12},{12,14},{14,16},{16,18},{18... | collective-permute-start | bytes 196616 | tf_op jit(solution)/shard_map/ppermute | solution.py:19
  41.6 10.4 %collective-permute-start.7 = (bf16[1,128,1,256]{1,3,2,0:T(8,128)(2,1)S(1)}, bf16[1,128,1,256]{1,3,2,0:T(8,128)(2,1)S(1)}, u32[]{:S(2)}, u32[]{:S(2)}) collective-permute-start(bf16[1,128,1,256]{1,3,2,0:T(8,128)(2,1)S(1)} %get-tuple-element.38), channel_id=1, source_target_pairs={{2,0},{4,2},{6,4},{8,6},{10,8},{12,10},{14,12},{16,14},{18,16},{20... | collective-permute-start | bytes 196616 | tf_op jit(solution)/shard_map/ppermute | solution.py:22
  46.0 49.1 %collective-permute-start.2 = (bf16[1,128,2,256]{1,3,2,0:T(8,128)(2,1)S(1)}, bf16[1,128,2,256]{1,3,2,0:T(8,128)(2,1)S(1)}, u32[]{:S(2)}, u32[]{:S(2)}) collective-permute-start(bf16[1,128,2,256]{1,3,2,0:T(8,128)(2,1)S(1)} %get-tuple-element.39), channel_id=1, source_target_pairs={{0,2},{2,4},{4,6},{6,8},{8,10},{10,12},{12,14},{14,16},{16,18},{18... | collective-permute-start | bytes 393224 | tf_op jit(solution)/shard_map/ppermute | solution.py:19
  46.0 49.1 %collective-permute-start.3 = (bf16[1,128,2,256]{1,3,2,0:T(8,128)(2,1)S(1)}, bf16[1,128,2,256]{1,3,2,0:T(8,128)(2,1)S(1)}, u32[]{:S(2)}, u32[]{:S(2)}) collective-permute-start(bf16[1,128,2,256]{1,3,2,0:T(8,128)(2,1)S(1)} %get-tuple-element.40), channel_id=1, source_target_pairs={{2,0},{4,2},{6,4},{8,6},{10,8},{12,10},{14,12},{16,14},{18,16},{20... | collective-permute-start | bytes 393224 | tf_op jit(solution)/shard_map/ppermute | solution.py:22
  54.8 2.2 copy-start.21
  95.1 0.7 copy-start.11
  95.1 0.7 copy-start.13
  100.6 1.0 copy-start.20
  103.8 2.3 copy-start.14
  105.1 1.4 copy-start.6
  105.1 1.4 copy-start.7
  105.1 1.4 copy-start.12
  106.0 0.8 copy-start.4
  106.1 0.9 copy-start.5
  106.1 0.9 copy-start.8
  106.1 226.3 %all-reduce.9.cloned.1.call-start = ((), (), s32[]{:S(2)}) async-start(), calls=%async_computation.1 | async-start | bytes 2359296 | tf_op jit(solution)/shard_map/psum | solution.py:172
  108.5 11.9 %copy-start.9 = (bf16[2,128,128]{2,1,0:T(8,128)(2,1)S(1)}, bf16[2,128,128]{2,1,0:T(8,128)(2,1)}, u32[]{:S(2)}) copy-start(bf16[2,128,128]{2,1,0:T(8,128)(2,1)} %all_gather.7) | copy-start | bytes 196612
  332.4 2.0 copy-start.3
  (1 other events, 0.6 us)
Sparse Core Ops, SparseCore 0:
  106.2 86.2 all-reduce.6
  199.5 132.8 all-reduce.8
where the time goes:
time: 343 us; the launch traced here: 342 us
  waiting for transfers between devices  209 us (61%)
  blocking collectives  53.6 us (16%)
  matrix products  19.5 us (6%)
  starting transfers between devices  19 us (6%)
  other arithmetic  15.1 us (4%)
  between operations  14.6 us (4%)
  local copies, waits for them, and re-layouts  11 us (3%)
    psum x1, waiting for transfers between devices, shards(): lax.psum((second_kernel_partial, first_kernel_partial, input_local, embed...  138 us
    psum x1, waiting for transfers between devices, shards(): join_total = lax.psum(join_local, 'az')  70.7 us
    psum x1, blocking collectives, shards(): lax.psum((second_kernel_partial, first_kernel_partial, input_local, embed...  37.2 us
    ppermute x4, starting transfers between devices, padded_2(): lax.ppermute(lax.slice_in_dim(block, 0, width, axis=dim), axis, backward)  18.3 us
    all_gather x1, blocking collectives, shards(): lax.all_gather(final_state[None], 'el', axis=0, tiled=True)  11.7 us
    dot_general x18, matrix products, kernel_gradient_of(): jnp.einsum('niar,noar->io', window, upstream, preferred_element_type=jnp....  8.68 us
  transfers between devices with their start and end apart: 10, of which 2 were waited for; matrix products, arithmetic and copies ran while one was open for 5% of the time, Pallas kernels for 0%

commit v1 on v0

--- a/solution.py
+++ b/solution.py
@@ -135,7 +135,8 @@
     join_local = jnp.einsum(
         "biar,boar->io", final_state, joined_back, preferred_element_type=jnp.float32
     )
-    join_total = lax.psum(join_local, "az")
+    parts = lax.all_gather(join_local, "az", axis=0, tiled=False)
+    join_total = parts.sum(axis=0)
     grad_two = jnp.einsum(
         "io,boar->biar", group_weight, joined_back, preferred_element_type=jnp.float32
     )

time: 343 us -> 209 us (0.61)
  waiting for transfers between devices: 209 us -> 74.6 us
    psum x1 -> x0, waiting for transfers between devices: 70.7 us -> none  [shards(): join_total = lax.psum(join_local, 'az')]
    psum x1, waiting for transfers between devices: 138 us -> 74.6 us  [shards(): lax.psum((second_kernel_partial, first_kernel_partial, input_local, embed...]
  transfers between devices with their start and end apart: 10 -> 10, of which waited for: 2 -> 1; matrix products, arithmetic and copies ran while one was open for 5% -> 9% of each run, Pallas kernels for 0% -> 0%
where the time goes in v1:
time: 209 us; the launch traced here: 208 us
  waiting for transfers between devices  74.6 us (36%)
  blocking collectives  54.4 us (26%)
  matrix products  20.1 us (10%)
  starting transfers between devices  19 us (9%)
  between operations  16.1 us (8%)
  other arithmetic  13.9 us (7%)
  local copies, waits for them, and re-layouts  10.2 us (5%)
    psum x1, waiting for transfers between devices, shards(): lax.psum((second_kernel_partial, first_kernel_partial, input_local, embed...  74.6 us
    psum x1, blocking collectives, shards(): lax.psum((second_kernel_partial, first_kernel_partial, input_local, embed...  37.4 us
    ppermute x4, starting transfers between devices, padded_2(): lax.ppermute(lax.slice_in_dim(block, 0, width, axis=dim), axis, backward)  18.3 us
    all_gather x1, blocking collectives, shards(): lax.all_gather(final_state[None], 'el', axis=0, tiled=True)  12.3 us
    dot_general x18, matrix products, kernel_gradient_of(): jnp.einsum('niar,noar->io', window, upstream, preferred_element_type=jnp....  9.3 us
    unnamed x55, local copies, waits for them, and re-layouts  5.09 us
    all_gather x1, blocking collectives, shards(): lax.all_gather(join_weight, 'el', axis=0, tiled=True)  4.68 us
    conv_general_dilated x4, matrix products, convolve_partial(): lax.conv_general_dilated(padded, kernel, (1, 1), 'VALID', rhs_dilation=(d...  4.5 us
  transfers between devices with their start and end apart: 10, of which 1 were waited for; matrix products, arithmetic and copies ran while one was open for 9% of the time, Pallas kernels for 0%

profile of v1, /device:TPU:0, one launch (start us, length us, event | category | flops | bytes accessed | tf_op | source)
XLA Modules:
  0.0 208.3 jit_solution(16677643427880231782)
XLA Ops:
  8.1 1.0 convert_reduce_fusion.1
  9.0 0.9 convolution_reduce_fusion
  10.0 1.9 fusion.30
  12.4 5.0 %collective-permute-start.1 = (bf16[1,128,1,256]{1,3,2,0:T(8,128)(2,1)S(1)}, bf16[1,128,1,256]{1,3,2,0:T(8,128)(2,1)S(1)}, u32[]{:S(2)}, u32[]{:S(2)}) collective-permute-start(bf16[1,128,1,256]{1,3,2,0:T(8,128)(2,1)S(1)} %get-tuple-element.42), channel_id=1, source_target_pairs={{2,0},{4,2},{6,4},{8,6},{10,8},{12,10},{14,12},{16,14},{18,16},{20... | collective-permute-start | bytes 196616 | tf_op jit(solution)/shard_map/ppermute | solution.py:22
  17.8 1.2 fusion.177
  19.0 4.4 %collective-permute-start.5 = (bf16[1,128,2,256]{1,3,2,0:T(8,128)(2,1)S(1)}, bf16[1,128,2,256]{1,3,2,0:T(8,128)(2,1)S(1)}, u32[]{:S(2)}, u32[]{:S(2)}) collective-permute-start(bf16[1,128,2,256]{1,3,2,0:T(8,128)(2,1)S(1)} %get-tuple-element.44), channel_id=1, source_target_pairs={{2,0},{4,2},{6,4},{8,6},{10,8},{12,10},{14,12},{16,14},{18,16},{20... | collective-permute-start | bytes 393224 | tf_op jit(solution)/shard_map/ppermute | solution.py:22
  23.4 4.7 %all_gather.13 = bf16[2,128,128]{2,1,0:T(8,128)(2,1)} all-gather(bf16[1,128,128]{2,1,0:T(8,128)(2,1)S(1)} %copy-done.13), channel_id=1, replica_groups=mesh['az'=16,'el'=2] {'el'}, dimensions={0}, use_global_device_ids=true | all-gather | bytes 98304 | tf_op jit(solution)/shard_map/all_gather | solution.py:121
  29.5 1.1 convolution_select_fusion.3
  30.8 1.0 reshape.191
  33.2 1.1 convolution_select_fusion.1
  34.5 1.0 reshape.195
  35.5 3.1 %fusion.170 = (bf16[1,128,6,256]{1,3,2,0:T(8,128)(2,1)S(1)}, f32[1,128,6,256]{1,3,2,0:T(8,128)}, bf16[1,128,6,256]{1,3,2,0:T(8,128)(2,1)S(1)}) fusion(f32[1,128,6,256]{1,3,2,0:T(8,128)} %get-tuple-element.46, f32[6,1,264,128]{3,2,0,1:T(8,128)} %reshape.195, f32[6,1,264,128]{3,2,0,1:T(8,128)} %reshape.191, f32[6,256,128]{2,1,0:T(8,128)} %get-tuple-element.48), kind=kLoop, calls=%fused_computation.226 | loop fusion | flops 2555904 | bytes 4718592 | tf_op jit(solution)/shard_map/convert_element_type | solution.py:154
  38.8 0.9 convolution_bitcast_fusion.6
  42.4 4.4 %collective-permute-start.7 = (bf16[1,128,1,256]{1,3,2,0:T(8,128)(2,1)S(1)}, bf16[1,128,1,256]{1,3,2,0:T(8,128)(2,1)S(1)}, u32[]{:S(2)}, u32[]{:S(2)}) collective-permute-start(bf16[1,128,1,256]{1,3,2,0:T(8,128)(2,1)S(1)} %get-tuple-element.38), channel_id=1, source_target_pairs={{2,0},{4,2},{6,4},{8,6},{10,8},{12,10},{14,12},{16,14},{18,16},{20... | collective-permute-start | bytes 196616 | tf_op jit(solution)/shard_map/ppermute | solution.py:22
  46.8 4.4 %collective-permute-start.3 = (bf16[1,128,2,256]{1,3,2,0:T(8,128)(2,1)S(1)}, bf16[1,128,2,256]{1,3,2,0:T(8,128)(2,1)S(1)}, u32[]{:S(2)}, u32[]{:S(2)}) collective-permute-start(bf16[1,128,2,256]{1,3,2,0:T(8,128)(2,1)S(1)} %get-tuple-element.40), channel_id=1, source_target_pairs={{2,0},{4,2},{6,4},{8,6},{10,8},{12,10},{14,12},{16,14},{18,16},{20... | collective-permute-start | bytes 393224 | tf_op jit(solution)/shard_map/ppermute | solution.py:22
  51.9 0.9 pad_maximum_fusion.1
  53.4 1.1 convolution_select_fusion
  54.7 1.0 reshape.197
  56.3 0.9 convolution_bitcast_fusion.5
  57.3 0.9 convolution_bitcast_fusion.7
  58.2 0.9 convolution_bitcast_fusion.8
  59.1 0.9 convolution_bitcast_fusion.2
  60.1 0.9 convolution_bitcast_fusion.4
  64.3 1.1 convolution_select_fusion.2
  65.8 0.9 convolution_bitcast_fusion.20
  67.1 1.5 convert_reduce_fusion
  69.1 37.4 %all-reduce.2 = (f32[24,128]{1,0:T(8,128)S(1)}, f32[4,128]{1,0:T(4,128)S(1)}) all-reduce(f32[24,128]{1,0:T(8,128)S(1)} %convolution_bitcast_fusion.21, f32[4,128]{1,0:T(4,128)S(1)} %fusion.135), channel_id=1, replica_groups=mesh['az'=16,'el'=2] {'az','el'}, use_global_device_ids=true, to_apply=%region_5.6 | all-reduce | flops 3584 | bytes 28672 | tf_op jit(solution)/shard_map/psum | solution.py:173
  107.8 12.3 %all-gather = bf16[2,128,6,256]{3,1,2,0:T(8,128)(2,1)S(1)} all-gather(bf16[1,128,6,256]{3,1,2,0:T(8,128)(2,1)S(1)} %copy.130), channel_id=2, replica_groups=mesh['az'=16,'el'=2] {'el'}, dimensions={0}, use_global_device_ids=true | all-gather | bytes 1179648 | tf_op jit(solution)/shard_map/all_gather | solution.py:120
  121.5 74.6 %all-reduce.6.cloned.1.call-done = (f32[3,3,128,128]{3,2,1,0:T(8,128)}, f32[3,3,128,128]{3,2,1,0:T(8,128)}) async-done(((f32[3,3,128,128]{3,2,1,0:T(8,128)}, f32[3,3,128,128]{3,2,1,0:T(8,128)}), (f32[3,3,128,128]{3,2,1,0:T(8,128)}, f32[3,3,128,128]{3,2,1,0:T(8,128)})) %all-reduce.6.cloned.1.call-update) | async-done | bytes 1179664 | tf_op jit(solution)/shard_map/psum | solution.py:173
  196.1 2.0 broadcast_multiply_fusion
  198.1 0.9 broadcast_multiply_fusion.1
  199.0 1.3 reduce_sum.42
  (126 shorter events, 16.6 us)
Async XLA Ops:
  8.0 20.9 %copy-start = (bf16[3,3,128,128]{3,2,1,0:T(8,128)(2,1)S(1)}, bf16[3,3,128,128]{3,2,1,0:T(8,128)(2,1)}, u32[]{:S(2)}) copy-start(bf16[3,3,128,128]{3,2,1,0:T(8,128)(2,1)} %param.13) | copy-start | bytes 884740
  8.0 188.1 %all-reduce.6.cloned.1.call-start = ((), (), s32[]{:S(2)}) async-start(), calls=%async_computation.1 | async-start | bytes 2359296 | tf_op jit(solution)/shard_map/psum | solution.py:173
  9.9 7.5 %copy-start.20 = (bf16[1,12,6,256]{3,2,1,0:T(8,128)(2,1)S(1)}, bf16[1,12,6,256]{3,2,1,0:T(8,128)(2,1)}, u32[]{:S(2)}) copy-start(bf16[1,12,6,256]{3,2,1,0:T(8,128)(2,1)} %param.17) | copy-start | bytes 110596
  9.9 7.5 %copy-start.21 = (bf16[12,128]{1,0:T(8,128)(2,1)S(1)}, bf16[12,128]{1,0:T(8,128)(2,1)}, u32[]{:S(2)}) copy-start(bf16[12,128]{1,0:T(8,128)(2,1)} %param.16) | copy-start | bytes 9220
  9.9 7.8 %copy-start.13 = (bf16[1,128,128]{2,1,0:T(8,128)(2,1)S(1)}, bf16[1,128,128]{2,1,0:T(8,128)(2,1)}, u32[]{:S(2)}) copy-start(bf16[1,128,128]{2,1,0:T(8,128)(2,1)} %param.15) | copy-start | bytes 98308
  11.9 16.2 %copy-start.3 = (bf16[128,6,256]{0,2,1:T(8,128)(2,1)}, bf16[128,6,256]{0,2,1:T(8,128)(2,1)S(1)}, u32[]{:S(2)}) copy-start(bf16[128,6,256]{0,2,1:T(8,128)(2,1)S(1)} %get-tuple-element.47) | copy-start | bytes 1179652
  11.9 16.2 %collective-permute-start = (bf16[1,128,1,256]{1,3,2,0:T(8,128)(2,1)S(1)}, bf16[1,128,1,256]{1,3,2,0:T(8,128)(2,1)S(1)}, u32[]{:S(2)}, u32[]{:S(2)}) collective-permute-start(bf16[1,128,1,256]{1,3,2,0:T(8,128)(2,1)S(1)} %get-tuple-element.41), channel_id=1, source_target_pairs={{0,2},{2,4},{4,6},{6,8},{8,10},{10,12},{12,14},{14,16},{16,18},{18... | collective-permute-start | bytes 196616 | tf_op jit(solution)/shard_map/ppermute | solution.py:19
  12.4 15.7 %collective-permute-start.1 = (bf16[1,128,1,256]{1,3,2,0:T(8,128)(2,1)S(1)}, bf16[1,128,1,256]{1,3,2,0:T(8,128)(2,1)S(1)}, u32[]{:S(2)}, u32[]{:S(2)}) collective-permute-start(bf16[1,128,1,256]{1,3,2,0:T(8,128)(2,1)S(1)} %get-tuple-element.42), channel_id=1, source_target_pairs={{2,0},{4,2},{6,4},{8,6},{10,8},{12,10},{14,12},{16,14},{18,16},{20... | collective-permute-start | bytes 196616 | tf_op jit(solution)/shard_map/ppermute | solution.py:22
  18.9 12.8 %collective-permute-start.4 = (bf16[1,128,2,256]{1,3,2,0:T(8,128)(2,1)S(1)}, bf16[1,128,2,256]{1,3,2,0:T(8,128)(2,1)S(1)}, u32[]{:S(2)}, u32[]{:S(2)}) collective-permute-start(bf16[1,128,2,256]{1,3,2,0:T(8,128)(2,1)S(1)} %get-tuple-element.43), channel_id=1, source_target_pairs={{0,2},{2,4},{4,6},{6,8},{8,10},{10,12},{12,14},{14,16},{16,18},{18... | collective-permute-start | bytes 393224 | tf_op jit(solution)/shard_map/ppermute | solution.py:19
  19.0 12.7 %collective-permute-start.5 = (bf16[1,128,2,256]{1,3,2,0:T(8,128)(2,1)S(1)}, bf16[1,128,2,256]{1,3,2,0:T(8,128)(2,1)S(1)}, u32[]{:S(2)}, u32[]{:S(2)}) collective-permute-start(bf16[1,128,2,256]{1,3,2,0:T(8,128)(2,1)S(1)} %get-tuple-element.44), channel_id=1, source_target_pairs={{2,0},{4,2},{6,4},{8,6},{10,8},{12,10},{14,12},{16,14},{18,16},{20... | collective-permute-start | bytes 393224 | tf_op jit(solution)/shard_map/ppermute | solution.py:22
  32.2 1.0 copy-start.22
  40.3 1.0 copy-start.4
  41.7 9.6 %copy-start.19 = (bf16[1,128,1,256]{1,3,2,0:T(8,128)(2,1)S(1)}, bf16[1,128,1,256]{1,3,2,0:T(8,128)(2,1)}, u32[]{:S(2)}) copy-start(bf16[1,128,1,256]{1,3,2,0:T(8,128)(2,1)} %copy-done.18) | copy-start | bytes 196612
  42.3 10.5 %collective-permute-start.6 = (bf16[1,128,1,256]{1,3,2,0:T(8,128)(2,1)S(1)}, bf16[1,128,1,256]{1,3,2,0:T(8,128)(2,1)S(1)}, u32[]{:S(2)}, u32[]{:S(2)}) collective-permute-start(bf16[1,128,1,256]{1,3,2,0:T(8,128)(2,1)S(1)} %get-tuple-element.37), channel_id=1, source_target_pairs={{0,2},{2,4},{4,6},{6,8},{8,10},{10,12},{12,14},{14,16},{16,18},{18... | collective-permute-start | bytes 196616 | tf_op jit(solution)/shard_map/ppermute | solution.py:19
  42.4 10.4 %collective-permute-start.7 = (bf16[1,128,1,256]{1,3,2,0:T(8,128)(2,1)S(1)}, bf16[1,128,1,256]{1,3,2,0:T(8,128)(2,1)S(1)}, u32[]{:S(2)}, u32[]{:S(2)}) collective-permute-start(bf16[1,128,1,256]{1,3,2,0:T(8,128)(2,1)S(1)} %get-tuple-element.38), channel_id=1, source_target_pairs={{2,0},{4,2},{6,4},{8,6},{10,8},{12,10},{14,12},{16,14},{18,16},{20... | collective-permute-start | bytes 196616 | tf_op jit(solution)/shard_map/ppermute | solution.py:22
  46.8 8.8 %collective-permute-start.2 = (bf16[1,128,2,256]{1,3,2,0:T(8,128)(2,1)S(1)}, bf16[1,128,2,256]{1,3,2,0:T(8,128)(2,1)S(1)}, u32[]{:S(2)}, u32[]{:S(2)}) collective-permute-start(bf16[1,128,2,256]{1,3,2,0:T(8,128)(2,1)S(1)} %get-tuple-element.39), channel_id=1, source_target_pairs={{0,2},{2,4},{4,6},{6,8},{8,10},{10,12},{12,14},{14,16},{16,18},{18... | collective-permute-start | bytes 393224 | tf_op jit(solution)/shard_map/ppermute | solution.py:19
  46.8 8.8 %collective-permute-start.3 = (bf16[1,128,2,256]{1,3,2,0:T(8,128)(2,1)S(1)}, bf16[1,128,2,256]{1,3,2,0:T(8,128)(2,1)S(1)}, u32[]{:S(2)}, u32[]{:S(2)}) collective-permute-start(bf16[1,128,2,256]{1,3,2,0:T(8,128)(2,1)S(1)} %get-tuple-element.40), channel_id=1, source_target_pairs={{2,0},{4,2},{6,4},{8,6},{10,8},{12,10},{14,12},{16,14},{18,16},{20... | collective-permute-start | bytes 393224 | tf_op jit(solution)/shard_map/ppermute | solution.py:22
  61.4 0.9 copy-start.17
  61.4 1.2 copy-start.9
  61.4 1.2 copy-start.10
  61.5 1.1 copy-start.15
  62.3 0.9 copy-start.6
  62.3 0.9 copy-start.7
  62.3 0.9 copy-start.8
  62.3 0.9 copy-start.11
  63.3 1.0 copy-start.23
  64.2 134.8 %all-gather.4.cloned.1.call-start = ((), (), s32[]{:S(2)}) async-start(), calls=%async_computation | async-start | bytes 1114112 | tf_op jit(solution)/shard_map/all_gather | solution.py:138
  65.7 1.1 copy-start.1
  65.8 1.3 copy-start.2
  67.1 1.7 copy-start.24
  68.8 51.3 %copy-start.12 = (bf16[2,128,128]{2,1,0:T(8,128)(2,1)S(1)}, bf16[2,128,128]{2,1,0:T(8,128)(2,1)}, u32[]{:S(2)}) copy-start(bf16[2,128,128]{2,1,0:T(8,128)(2,1)} %all_gather.13) | copy-start | bytes 196612
  196.1 2.0 copy-start.5
  (4 other events, 2.7 us)
Sparse Core Ops, SparseCore 0:
  64.3 131.7 all-reduce.5
Sparse Core Ops, SparseCore 1:
  67.4 38.3 all-gather.3
